TPU v7x, 32 devices: a whole 2x2x4 slice. The times are simulated.
32 devices in a mesh: dp: 4 (over y, x), mx: 4 (over z), my: 2 (over core).
Axes of the slice: x: 2, y: 2, z: 4, core: 2. Of those that a mesh axis runs over, the one named last changes fastest.
Arguments:
- tokens: bfloat16 [8192, 2048], P(('dp', 'my'), 'mx'), may hold values from -6 to 6
- output_grad: bfloat16 [8192, 2048], P(('dp', 'my'), 'mx'), may hold values from -6 to 6
- picture_starts: int32 [8, 2], P('dp'), may hold values from 0 to 768, as said below
- norm1_gain: float32 [2048], P('mx'), may hold values from 0.5 to 1.5
- query_weight: bfloat16 [2048, 2048], P('mx', 'my'), may hold values from -0.5 to 0.5
- key_weight: bfloat16 [2048, 512], P('mx', 'my'), may hold values from -0.5 to 0.5
- value_weight: bfloat16 [2048, 512], P('mx', 'my'), may hold values from -0.125 to 0.125
- out_weight: bfloat16 [2048, 2048], P('my', 'mx'), may hold values from -2 to 2
- norm2_gain: float32 [2048], P('mx'), may hold values from 0.5 to 1.5
- gate_weight: bfloat16 [2048, 8192], P('mx', 'my'), may hold values from -0.125 to 0.125
- up_weight: bfloat16 [2048, 8192], P('mx', 'my'), may hold values from -0.125 to 0.125
- down_weight: bfloat16 [8192, 2048], P('my', 'mx'), may hold values from -0.5 to 0.5
Outputs:
- output: bfloat16 [8192, 2048], P(('dp', 'my'), 'mx')
- input_grad: bfloat16 [8192, 2048], P(('dp', 'my'), 'mx')
- grad_norm1: float32 [2048], P('mx')
- grad_query: float32 [2048, 2048], P('mx', 'my')
- grad_key: float32 [2048, 512], P('mx', 'my')
- grad_value: float32 [2048, 512], P('mx', 'my')
- grad_out: float32 [2048, 2048], P('my', 'mx')
- grad_norm2: float32 [2048], P('mx')
- grad_gate: float32 [2048, 8192], P('mx', 'my')
- grad_up: float32 [2048, 8192], P('mx', 'my')
- grad_down: float32 [8192, 2048], P('my', 'mx')
Inputs may be any that keep to these rules, and one draw needn't show every extreme that they name: `picture_starts`: piece p of a sequence starts at a position from p * 512 to (p + 1) * 512 - 256, so the pieces of a sequence never intersect and lie inside it; some sequence has its first piece at position 0 and some sequence has its last piece ending at the sequence's end.
All inputs are finite; a program needn't handle non-finite values.
Results may differ from a plain program's by a relative error of at most 0.02.
Values may be sent and summed in bfloat16 or wider, within the bound.
No kernel may reach another device: no remote copies, remote signals or barrier semaphores. Data moves between devices by JAX's collectives and lax.ppermute only.
A program may use at most 384 MiB of HBM per device.

v0:
```python
import jax
import jax.numpy as jnp
from jax import lax
from jax.sharding import PartitionSpec as P

D = 2048
HEAD = 64
LEN = 1024
PIECE = 256
epsilon = 1e-05
rope_base = 10000000.0
branch_scale = 0.22
score_scale = 0.015625
masked_score = -1e30


def rope_tables(positions, head_width):
    half_width = head_width // 2
    steps_idx = jnp.arange(half_width, dtype=jnp.float32)
    freqs = jnp.exp(-jnp.log(jnp.float32(rope_base)) * 2.0 * steps_idx / head_width)
    angles = positions.astype(jnp.float32)[:, None] * freqs[None, :]
    cosine = jnp.cos(angles)
    sine = jnp.sin(angles)
    return (jnp.concatenate([cosine, cosine], 1), jnp.concatenate([sine, sine], 1))


def rotate_half(values):
    half_width = values.shape[-1] // 2
    return jnp.concatenate([-values[..., half_width:], values[..., :half_width]], -1)


def apply_rope(values, cosine, sine):
    return values * cosine + rotate_half(values) * sine


def rope_back(values, cosine, sine):
    return values * cosine - rotate_half(values) * sine


def product(left, weight, flipped):
    if flipped:
        return lax.dot_general(
            left, weight, (((1,), (1,)), ((), ())), preferred_element_type=jnp.float32
        )
    return jnp.dot(left, weight, preferred_element_type=jnp.float32)


def outer_sum(left, right):
    return lax.dot_general(
        left, right, (((0,), (0,)), ((), ())), preferred_element_type=jnp.float32
    )


def head_scores(query, key_head, allowed_pairs):
    scores = (
        jnp.einsum("qgd,kd->qgk", query, key_head, preferred_element_type=jnp.float32) * score_scale
    )
    return jnp.where(allowed_pairs[:, None, :], scores, masked_score)


def head_forward(query, key_head, value_head, allowed_pairs):
    scores = head_scores(query, key_head, allowed_pairs)
    row_max = jnp.max(scores, axis=-1, keepdims=True)
    shifted = jnp.exp(scores - row_max)
    row_total = jnp.sum(shifted, axis=-1, keepdims=True)
    probs = shifted / row_total
    mixed = jnp.einsum(
        "qgk,kd->qgd", probs.astype(jnp.bfloat16), value_head, preferred_element_type=jnp.float32
    )
    return (mixed, (row_max + jnp.log(row_total))[..., 0])


def head_backward(query, key_head, value_head, grad_out, log_total, allowed_pairs):
    scores = head_scores(query, key_head, allowed_pairs)
    probs = jnp.exp(scores - log_total[..., None])
    grad_probs = jnp.einsum("qgd,kd->qgk", grad_out, value_head, preferred_element_type=jnp.float32)
    row_dot = jnp.sum(probs * grad_probs, axis=-1, keepdims=True)
    grad_scores = (probs * (grad_probs - row_dot)).astype(jnp.bfloat16)
    grad_query = (
        jnp.einsum("qgk,kd->qgd", grad_scores, key_head, preferred_element_type=jnp.float32)
        * score_scale
    )
    grad_key = (
        jnp.einsum("qgk,qgd->kd", grad_scores, query, preferred_element_type=jnp.float32)
        * score_scale
    )
    grad_value = jnp.einsum(
        "qgk,qgd->kd", probs.astype(jnp.bfloat16), grad_out, preferred_element_type=jnp.float32
    )
    return (grad_query, grad_key, grad_value)


PLANE = ("dp", "my")


def plane_gather(values):
    return lax.all_gather(values, PLANE, axis=0, tiled=True)


def plane_scatter(values):
    return lax.psum_scatter(
        values.astype(jnp.bfloat16), PLANE, scatter_dimension=0, tiled=True
    ).astype(jnp.float32)


def to_rows(values):
    return lax.all_to_all(values, "mx", split_axis=0, concat_axis=1, tiled=True)


def to_tiles(values):
    return lax.all_to_all(values, "mx", split_axis=1, concat_axis=0, tiled=True)


def line_gather(values, axis):
    return lax.all_gather(values, "mx", axis=axis, tiled=True)


def line_scatter(values, axis):
    return lax.psum_scatter(values.astype(jnp.bfloat16), "mx", scatter_dimension=axis, tiled=True)


def norm_forward(stream, gain):
    mean = jnp.mean(stream * stream, axis=1, keepdims=True)
    inverse = lax.rsqrt(mean + epsilon)
    return (inverse, (stream * inverse * gain[None, :]).astype(jnp.bfloat16))


def norm_backward(stream, inverse, gain, grad_normed):
    scaled = gain[None, :] * grad_normed
    row_mean = jnp.mean(stream * scaled, axis=1, keepdims=True)
    grad_stream = inverse * scaled - stream * inverse * inverse * inverse * row_mean
    grad_gain = jnp.sum(grad_normed * stream * inverse, axis=0)
    return (grad_stream, grad_gain)


def piece_of(position, begins):
    inside = (position >= begins) & (position < begins + PIECE)
    number = jnp.arange(1, begins.shape[-1] + 1, dtype=jnp.int32)
    return jnp.sum(jnp.where(inside, number, 0), axis=-1)


def shards(
    tokens,
    output_grad,
    picture_starts,
    norm1_gain,
    query_weight,
    key_weight,
    value_weight,
    out_weight,
    norm2_gain,
    gate_weight,
    up_weight,
    down_weight,
):
    mx_count = lax.axis_size("mx")
    dp_count = lax.axis_size("dp")
    dp_index = lax.axis_index("dp")
    mx_index = lax.axis_index("mx")
    chunk = LEN // mx_count
    seqs = dp_count * lax.axis_size("my")
    rows = seqs * chunk
    query_cols = query_weight.shape[1] // dp_count
    query_heads = query_cols // HEAD
    key_heads = key_weight.shape[1] // HEAD
    share = max(1, dp_count // key_heads)
    key_cols = key_weight.shape[1] * share // dp_count
    own_keys = key_cols // HEAD
    kv_group = query_heads // own_keys
    hidden = gate_weight.shape[1] // dp_count

    def cols(weight, width, index):
        return lax.dynamic_slice_in_dim(weight, index * width, width, axis=1)

    def rows_of(weight, width):
        return lax.dynamic_slice_in_dim(weight, dp_index * width, width, axis=0)

    key_index = dp_index // share
    attn_in = line_gather(
        jnp.concatenate(
            [
                cols(query_weight, query_cols, dp_index),
                cols(key_weight, key_cols, key_index),
                cols(value_weight, key_cols, key_index),
            ],
            axis=1,
        ),
        0,
    )
    attn_back = line_gather(rows_of(out_weight, query_cols), 1)
    ffn_in = line_gather(
        jnp.concatenate(
            [cols(gate_weight, hidden, dp_index), cols(up_weight, hidden, dp_index)], axis=1
        ),
        0,
    )
    ffn_back = line_gather(rows_of(down_weight, hidden), 1)
    gains = line_gather(jnp.stack([norm1_gain, norm2_gain]), 1)
    gain_one, gain_two = (gains[0], gains[1])
    starts = lax.all_gather(picture_starts, "dp", axis=0, tiled=True)
    stream = to_rows(tokens).astype(jnp.float32)
    grad_two = to_rows(output_grad).astype(jnp.float32)
    inverse_one, normed_one = norm_forward(stream, gain_one)
    normed_one_all = plane_gather(normed_one)
    projected = product(normed_one_all, attn_in, False)
    query_pos = mx_index * chunk + jnp.arange(chunk, dtype=jnp.int32)
    key_pos = jnp.arange(LEN, dtype=jnp.int32)
    cosine, sine = rope_tables(query_pos, HEAD)
    cosine = cosine[None, :, None, :]
    sine = sine[None, :, None, :]
    query_piece = piece_of(query_pos[None, :, None], starts[:, None, :])
    key_piece = piece_of(key_pos[None, :, None], starts[:, None, :])
    before = key_pos[None, None, :] <= query_pos[None, :, None]
    same = (query_piece[:, :, None] > 0) & (query_piece[:, :, None] == key_piece[:, None, :])
    allowed_pairs = before | same
    query_rot = apply_rope(
        projected[:, :query_cols].reshape(seqs, chunk, query_heads, HEAD), cosine, sine
    ).astype(jnp.bfloat16)
    key_rot = apply_rope(
        projected[:, query_cols : query_cols + key_cols].reshape(seqs, chunk, own_keys, HEAD),
        cosine,
        sine,
    ).astype(jnp.bfloat16)
    value_own = projected[:, query_cols + key_cols :].astype(jnp.bfloat16)
    key_local = jnp.concatenate(
        [key_rot.reshape(seqs, chunk, key_cols), value_own.reshape(seqs, chunk, key_cols)], axis=2
    )
    key_all = line_gather(key_local, 1)
    query_split = query_rot.reshape(seqs, chunk, own_keys, kv_group, HEAD)
    query_split = query_split.transpose(0, 2, 1, 3, 4).reshape(-1, chunk, kv_group, HEAD)

    def split_keys(values):
        values = values.reshape(seqs, LEN, own_keys, HEAD)
        return values.transpose(0, 2, 1, 3).reshape(-1, LEN, HEAD)

    key_split = split_keys(key_all[:, :, :key_cols])
    value_split = split_keys(key_all[:, :, key_cols:])
    pairs = jnp.repeat(allowed_pairs, own_keys, axis=0)
    mixed, log_totals = lax.map(
        lambda p: head_forward(p[0], p[1], p[2], p[3]), (query_split, key_split, value_split, pairs)
    )

    def join_heads(values):
        values = values.reshape(seqs, own_keys, chunk, kv_group, HEAD).transpose(0, 2, 1, 3, 4)
        return values.reshape(rows, query_cols)

    def split_heads(values):
        values = values.reshape(seqs, chunk, own_keys, kv_group, HEAD).transpose(0, 2, 1, 3, 4)
        return values.reshape(-1, chunk, kv_group, HEAD)

    attn_out = join_heads(mixed).astype(jnp.bfloat16)
    hidden_one = stream + branch_scale * plane_scatter(product(attn_out, attn_back, False))
    inverse_two, normed_two = norm_forward(hidden_one, gain_two)
    normed_two_all = plane_gather(normed_two)
    gate_up = product(normed_two_all, ffn_in, False)
    gate_val = gate_up[:, :hidden]
    up_val = gate_up[:, hidden:]
    sigma = jax.nn.sigmoid(gate_val)
    silu_gate = gate_val * sigma
    hidden_units = (silu_gate * up_val).astype(jnp.bfloat16)
    hidden_two = hidden_one + branch_scale * plane_scatter(product(hidden_units, ffn_back, False))
    output = to_tiles(hidden_two.astype(jnp.bfloat16))
    branch_two = (branch_scale * grad_two).astype(jnp.bfloat16)
    branch_two_all = plane_gather(branch_two)
    grad_down = outer_sum(hidden_units, branch_two_all)
    grad_hidden = product(branch_two_all, ffn_back, True)
    grad_gate_val = (grad_hidden * up_val * sigma * (1.0 + gate_val * (1.0 - sigma))).astype(
        jnp.bfloat16
    )
    grad_up_val = (grad_hidden * silu_gate).astype(jnp.bfloat16)
    grad_gate_up = jnp.concatenate([grad_gate_val, grad_up_val], axis=1)
    grad_ffn_in = outer_sum(normed_two_all, grad_gate_up)
    grad_normed_two = plane_scatter(product(grad_gate_up, ffn_in, True))
    grad_stream_two, grad_norm2 = norm_backward(hidden_one, inverse_two, gain_two, grad_normed_two)
    grad_one = grad_two + grad_stream_two
    branch_one_all = plane_gather((branch_scale * grad_one).astype(jnp.bfloat16))
    grad_out = outer_sum(attn_out, branch_one_all)
    grad_attn = split_heads(product(branch_one_all, attn_back, True).astype(jnp.bfloat16))
    grad_q, grad_k, grad_v = lax.map(
        lambda p: head_backward(p[0], p[1], p[2], p[3], p[4], p[5]),
        (query_split, key_split, value_split, grad_attn, log_totals, pairs),
    )

    def join_keys(values):
        values = values.reshape(seqs, own_keys, LEN, HEAD).transpose(0, 2, 1, 3)
        return values.reshape(seqs, LEN, key_cols)

    key_terms = jnp.concatenate([join_keys(grad_k), join_keys(grad_v)], axis=2)
    key_owned = line_scatter(key_terms, 1).astype(jnp.float32)
    grad_q_pre = rope_back(join_heads(grad_q).reshape(seqs, chunk, query_heads, HEAD), cosine, sine)
    grad_k_pre = rope_back(
        key_owned[:, :, :key_cols].reshape(seqs, chunk, own_keys, HEAD), cosine, sine
    )
    grad_projected = jnp.concatenate(
        [
            grad_q_pre.reshape(rows, query_cols),
            grad_k_pre.reshape(rows, key_cols),
            key_owned[:, :, key_cols:].reshape(rows, key_cols),
        ],
        axis=1,
    ).astype(jnp.bfloat16)
    grad_attn_in = outer_sum(normed_one_all, grad_projected)
    grad_normed_one = plane_scatter(product(grad_projected, attn_in, True))
    grad_stream_one, grad_norm1 = norm_backward(stream, inverse_one, gain_one, grad_normed_one)
    input_grad = to_tiles((grad_one + grad_stream_one).astype(jnp.bfloat16))

    def spread_cols(own):
        return lax.all_gather(own, "dp", axis=1, tiled=True).astype(jnp.float32)

    def spread_rows(own):
        return lax.all_gather(own, "dp", axis=0, tiled=True).astype(jnp.float32)

    def spread_keys(own):
        every = lax.all_gather(own, "dp", axis=0).astype(jnp.float32)
        every = every.reshape(dp_count // share, share, -1, key_cols).sum(axis=1)
        return every.transpose(1, 0, 2).reshape(every.shape[1], -1)

    grad_down = spread_rows(line_scatter(grad_down, 1))
    own_ffn = line_scatter(grad_ffn_in, 0)
    grad_gate = spread_cols(own_ffn[:, :hidden])
    grad_up = spread_cols(own_ffn[:, hidden:])
    grad_out = spread_rows(line_scatter(grad_out, 1))
    own_attn = line_scatter(grad_attn_in, 0)
    grad_query = spread_cols(own_attn[:, :query_cols])
    grad_key = spread_keys(own_attn[:, query_cols : query_cols + key_cols])
    grad_value = spread_keys(own_attn[:, query_cols + key_cols :])
    norms = lax.psum(jnp.stack([grad_norm1, grad_norm2]), ("dp", "mx", "my"))
    norms = lax.dynamic_slice_in_dim(norms, mx_index * norm1_gain.shape[0], norm1_gain.shape[0], 1)
    return (
        output,
        input_grad,
        norms[0],
        grad_query,
        grad_key,
        grad_value,
        grad_out,
        norms[1],
        grad_gate,
        grad_up,
        grad_down,
    )


def solution(mesh):
    placed = (
        P(("dp", "my"), "mx"),
        P(("dp", "my"), "mx"),
        P("dp", None),
        P("mx"),
        P("mx", "my"),
        P("mx", "my"),
        P("mx", "my"),
        P("my", "mx"),
        P("mx"),
        P("mx", "my"),
        P("mx", "my"),
        P("my", "mx"),
    )
    return jax.shard_map(
        shards,
        mesh=mesh,
        in_specs=placed,
        out_specs=(
            P(("dp", "my"), "mx"),
            P(("dp", "my"), "mx"),
            P("mx"),
            P("mx", "my"),
            P("mx", "my"),
            P("mx", "my"),
            P("my", "mx"),
            P("mx"),
            P("mx", "my"),
            P("mx", "my"),
            P("my", "mx"),
        ),
        check_vma=False,
    )
```

profile of v0, /device:TPU:0, one launch (start us, length us, event | category | flops | bytes accessed | tf_op | source)
XLA Modules:
  0.0 1764.2 jit_solution(13706677136220090018)
XLA Ops:
  15.8 45.3 %all_gather.61 = f32[2,2048]{1,0:T(2,128)S(1)} all-gather(f32[2,512]{1,0:T(2,128)S(1)} %pad_maximum_fusion.10), channel_id=1, replica_groups=mesh['dp'=4,'mx'=4,'my'=2] {'mx'}, dimensions={1}, use_global_device_ids=true | all-gather | bytes 20480 | tf_op jit(solution)/shard_map/all_gather | solution.py:115
  65.7 55.6 %all-gather.18.cloned.1.call-done = bf16[2048,2048]{1,0:T(8,128)(2,1)} async-done(((bf16[256,2048]{1,0:T(8,128)(2,1)}), bf16[2048,2048]{1,0:T(8,128)(2,1)}) %all-gather.18.cloned.1.call-update) | async-done | bytes 8388624 | tf_op jit(solution)/shard_map/all_gather | solution.py:97
  148.5 28.1 %all-gather.22.cloned.1.call-done = bf16[8,1024,128]{1,2,0:T(8,128)(2,1)} async-done(((bf16[8,256,128]{1,2,0:T(8,128)(2,1)}), bf16[8,1024,128]{1,2,0:T(8,128)(2,1)}) %all-gather.22.cloned.1.call-update) | async-done | bytes 2097168 | tf_op jit(solution)/shard_map/all_gather | solution.py:115
  179.7 57.7 %while.28 = (s32[]{:T(128)}, bf16[8,256,4,64]{1,3,2,0:T(8,128)(2,1)}, f32[8,256,4]{1,2,0:T(4,128)S(1)}, pred[8,256,1024]{2,1,0:T(8,128)(4,1)}, bf16[8,256,4,64]{...) while((s32[]{:T(128)}, bf16[8,256,4,64]{1,3,2,0:T(8,128)(2,1)}, ...), condition=%wide.region_6.7_spmd.clone, body=%wide.region_3.6_spmd.sunk.clone | while | flops 281017344 | bytes 14583893 | solution.py:239
  250.4 66.5 %reduce-scatter.10.cloned.1.call-done = bf16[256,2048]{1,0:T(8,128)(2,1)} async-done(((bf16[2048,2048]{1,0:T(8,128)(2,1)}), bf16[256,2048]{1,0:T(8,128)(2,1)}) %reduce-scatter.10.cloned.1.call-update) | async-done | bytes 1048592 | tf_op jit(solution)/shard_map/reduce_scatter | solution.py:101
  322.5 57.9 %all_to_all.64 = bf16[4,256,512]{2,1,0:T(8,128)(2,1)S(1)} all-to-all(bf16[4,256,512]{2,1,0:T(8,128)(2,1)} %bitcast.282), channel_id=1, replica_groups=mesh['dp'=4,'mx'=4,'my'=2] {'mx'}, dimensions={0} | all-to-all | bytes 2097152 | tf_op jit(solution)/shard_map/all_to_all | solution.py:107
  383.7 104.4 %all-gather.28.cloned.1.call-done = bf16[2048,2048]{1,0:T(8,128)(2,1)} async-done(((bf16[512,2048]{1,0:T(8,128)(2,1)}), bf16[2048,2048]{1,0:T(8,128)(2,1)}) %all-gather.28.cloned.1.call-update) | async-done | bytes 8388624 | tf_op jit(solution)/shard_map/all_gather | solution.py:115
  488.1 54.9 %all-gather.26.cloned.1.call-done = bf16[2048,2048]{1,0:T(8,128)(2,1)} async-done(((bf16[256,2048]{1,0:T(8,128)(2,1)}), bf16[2048,2048]{1,0:T(8,128)(2,1)}) %all-gather.26.cloned.1.call-update) | async-done | bytes 8388624 | tf_op jit(solution)/shard_map/all_gather | solution.py:97
  543.0 24.3 %fusion.93 = f32[2048,2048]{0,1:T(8,128)} fusion(bf16[2048,2048]{1,0:T(8,128)(2,1)} %all-gather.26.cloned.1.call-done, bf16[2048,2048]{1,0:T(8,128)(2,1)} %all-gather.28.cloned.1.call-done), kind=kOutput, calls=%fused_computation.183 | convolution fusion | flops 17179869184 | bytes 33554432 | tf_op jit(solution)/shard_map/dot_general | solution.py:45
  567.3 58.6 %all-gather.30.cloned.1.call-done = bf16[1024,2048]{1,0:T(8,128)(2,1)} async-done(((bf16[1024,512]{1,0:T(8,128)(2,1)}), bf16[1024,2048]{1,0:T(8,128)(2,1)}) %all-gather.30.cloned.1.call-update) | async-done | bytes 4194320 | tf_op jit(solution)/shard_map/all_gather | solution.py:115
  625.9 55.2 %all-gather.32.cloned.1.call-done = bf16[2048,2048]{1,0:T(8,128)(2,1)} async-done(((bf16[256,2048]{1,0:T(8,128)(2,1)}), bf16[2048,2048]{1,0:T(8,128)(2,1)}) %all-gather.32.cloned.1.call-update) | async-done | bytes 8388624 | tf_op jit(solution)/shard_map/all_gather | solution.py:97
  727.5 71.6 %reduce-scatter.14.cloned.1.call-done = bf16[256,2048]{1,0:T(8,128)(2,1)} async-done(((bf16[2048,2048]{1,0:T(8,128)(2,1)}), bf16[256,2048]{1,0:T(8,128)(2,1)}) %reduce-scatter.14.cloned.1.call-update) | async-done | bytes 1048592 | tf_op jit(solution)/shard_map/reduce_scatter | solution.py:101
  803.9 54.3 %all-gather.34.cloned.1.call-done = bf16[2048,2048]{1,0:T(8,128)(2,1)} async-done(((bf16[256,2048]{1,0:T(8,128)(2,1)}), bf16[2048,2048]{1,0:T(8,128)(2,1)}) %all-gather.34.cloned.1.call-update) | async-done | bytes 8388624 | tf_op jit(solution)/shard_map/all_gather | solution.py:97
  867.5 109.9 %while.29 = (s32[]{:T(128)}, f32[8,256,4,64]{1,3,2,0:T(8,128)}, bf16[8,1024,64]{1,2,0:T(8,128)(2,1)}, bf16[8,1024,64]{1,2,0:T(8,128)(2,1)}, pred[8,256,1024]{2,1...) while((s32[]{:T(128)}, f32[8,256,4,64]{1,3,2,0:T(8,128)}, ...), condition=%wide.region_14.15_spmd.clone, body=%wide.region_12.14_spmd.sunk.clone | while | flops 686947328 | bytes 34505836 | solution.py:279
  1064.5 38.1 %reduce-scatter.26.cloned.1.call-done = bf16[1024,512]{1,0:T(8,128)(2,1)} async-done(((bf16[1024,2048]{1,0:T(8,128)(2,1)}), bf16[1024,512]{1,0:T(8,128)(2,1)}) %reduce-scatter.26.cloned.1.call-update) | async-done | bytes 1048592 | tf_op jit(solution)/shard_map/reduce_scatter | solution.py:119
  1102.6 147.9 %reduce-scatter.24.cloned.1.call-done = bf16[512,2048]{1,0:T(8,128)(2,1)} async-done(((bf16[2048,2048]{1,0:T(8,128)(2,1)}), bf16[512,2048]{1,0:T(8,128)(2,1)}) %reduce-scatter.24.cloned.1.call-update) | async-done | bytes 2097168 | tf_op jit(solution)/shard_map/reduce_scatter | solution.py:119
  1254.3 26.2 %reduce-scatter.22.cloned.1.call-done = bf16[256,512]{1,0:T(8,128)(2,1)} async-done(((bf16[256,2048]{1,0:T(8,128)(2,1)}), bf16[256,512]{1,0:T(8,128)(2,1)}) %reduce-scatter.22.cloned.1.call-update) | async-done | bytes 262160 | tf_op jit(solution)/shard_map/reduce_scatter | solution.py:119
  1280.6 73.9 %reduce-scatter.18.cloned.1.call-done = bf16[256,2048]{1,0:T(8,128)(2,1)} async-done(((bf16[2048,2048]{1,0:T(8,128)(2,1)}), bf16[256,2048]{1,0:T(8,128)(2,1)}) %reduce-scatter.18.cloned.1.call-update) | async-done | bytes 1048592 | tf_op jit(solution)/shard_map/reduce_scatter | solution.py:101
  1356.4 73.5 %reduce-scatter.12.cloned.1.call-done = bf16[256,2048]{1,0:T(8,128)(2,1)} async-done(((bf16[2048,2048]{1,0:T(8,128)(2,1)}), bf16[256,2048]{1,0:T(8,128)(2,1)}) %reduce-scatter.12.cloned.1.call-update) | async-done | bytes 1048592 | tf_op jit(solution)/shard_map/reduce_scatter | solution.py:101
  1440.1 44.9 %reduce-scatter.20.cloned.1.call-done = bf16[512,384]{1,0:T(8,128)(2,1)} async-done(((bf16[2048,384]{1,0:T(8,128)(2,1)}), bf16[512,384]{1,0:T(8,128)(2,1)}) %reduce-scatter.20.cloned.1.call-update) | async-done | bytes 393232 | tf_op jit(solution)/shard_map/reduce_scatter | solution.py:119
  1495.3 47.7 %all-gather.44.cloned.1.call-done = bf16[4096,512]{1,0:T(8,128)(2,1)} async-done(((bf16[1024,512]{1,0:T(8,128)(2,1)}), bf16[4096,512]{1,0:T(8,128)(2,1)}) %all-gather.44.cloned.1.call-update) | async-done | bytes 4194320 | tf_op jit(solution)/shard_map/all_gather | solution.py:311
  1549.7 48.1 %all-gather.40.cloned.1.call-done = bf16[512,4096]{1,0:T(8,128)(2,1)} async-done(((bf16[512,1024]{1,0:T(8,128)(2,1)}), bf16[512,4096]{1,0:T(8,128)(2,1)}) %all-gather.40.cloned.1.call-update) | async-done | bytes 4194320 | tf_op jit(solution)/shard_map/all_gather | solution.py:308
  1604.5 48.4 %all-gather.42.cloned.1.call-done = bf16[512,4096]{1,0:T(8,128)(2,1)} async-done(((bf16[512,1024]{1,0:T(8,128)(2,1)}), bf16[512,4096]{1,0:T(8,128)(2,1)}) %all-gather.42.cloned.1.call-update) | async-done | bytes 4194320 | tf_op jit(solution)/shard_map/all_gather | solution.py:308
  1715.6 38.9 %psum.7 = f32[2,2048]{1,0:T(2,128)S(1)} all-reduce(f32[2,2048]{1,0:T(2,128)S(1)} %pad_maximum_fusion.9), channel_id=1, replica_groups=mesh['dp'=4,'mx'=4,'my'=2] {'dp','mx','my'}, use_global_device_ids=true, to_apply=%region_20.21 | all-reduce | flops 4096 | bytes 32768 | tf_op jit(solution)/shard_map/psum | solution.py:327
  (342 shorter events, 484.4 us)
Async XLA Ops:
  7.2 54.0 %all-to-all-start = ((bf16[4,256,512]{2,1,0:T(8,128)(2,1)}), bf16[4,256,512]{2,1,0:T(8,128)(2,1)S(1)}, u32[]{:S(2)}, u32[]{:S(2)}) async-start(bf16[4,256,512]{2,1,0:T(8,128)(2,1)} %bitcast.281), calls=%async_computation | async-start | bytes 2097152 | tf_op jit(solution)/shard_map/all_to_all | solution.py:107
  15.8 105.5 %all-gather.18.cloned.1.call-start = ((), (), s32[]{:S(2)}) async-start(), calls=%async_computation.13 | async-start | bytes 9437184 | tf_op jit(solution)/shard_map/all_gather | solution.py:97
  65.4 111.2 %all-gather.22.cloned.1.call-start = ((), (), s32[]{:S(2)}) async-start(), calls=%async_computation.15 | async-start | bytes 2621440 | tf_op jit(solution)/shard_map/all_gather | solution.py:115
  130.2 109.4 %all-gather.24.cloned.1.call-start = ((), (), s32[]{:S(2)}) async-start(), calls=%async_computation.16 | async-start | bytes 1310720 | tf_op jit(solution)/shard_map/all_gather | solution.py:115
  131.9 184.9 %reduce-scatter.10.cloned.1.call-start = ((), (), s32[]{:S(2)}) async-start(), calls=%async_computation.17 | async-start | bytes 9437184 | tf_op jit(solution)/shard_map/reduce_scatter | solution.py:101
  247.0 241.1 %all-gather.28.cloned.1.call-start = ((), (), s32[]{:S(2)}) async-start(), calls=%async_computation.19 | async-start | bytes 10485760 | tf_op jit(solution)/shard_map/all_gather | solution.py:115
  250.3 292.7 %all-gather.26.cloned.1.call-start = ((), (), s32[]{:S(2)}) async-start(), calls=%async_computation.18 | async-start | bytes 9437184 | tf_op jit(solution)/shard_map/all_gather | solution.py:97
  320.1 305.8 %all-gather.30.cloned.1.call-start = ((), (), s32[]{:S(2)}) async-start(), calls=%async_computation.20 | async-start | bytes 5242880 | tf_op jit(solution)/shard_map/all_gather | solution.py:115
  322.4 358.7 %all-gather.32.cloned.1.call-start = ((), (), s32[]{:S(2)}) async-start(), calls=%async_computation.22 | async-start | bytes 9437184 | tf_op jit(solution)/shard_map/all_gather | solution.py:97
  383.4 415.7 %reduce-scatter.14.cloned.1.call-start = ((), (), s32[]{:S(2)}) async-start(), calls=%async_computation.23 | async-start | bytes 9437184 | tf_op jit(solution)/shard_map/reduce_scatter | solution.py:101
  727.4 130.8 %all-gather.34.cloned.1.call-start = ((), (), s32[]{:S(2)}) async-start(), calls=%async_computation.24 | async-start | bytes 9437184 | tf_op jit(solution)/shard_map/all_gather | solution.py:97
  803.8 227.6 %reduce-scatter.16.cloned.1.call-start = ((), (), s32[]{:S(2)}) async-start(), calls=%async_computation.25 | async-start | bytes 2621440 | tf_op jit(solution)/shard_map/reduce_scatter | solution.py:119
  980.4 122.1 %reduce-scatter.26.cloned.1.call-start = ((), (), s32[]{:S(2)}) async-start(), calls=%async_computation.34 | async-start | bytes 5242880 | tf_op jit(solution)/shard_map/reduce_scatter | solution.py:119
  994.4 256.1 %reduce-scatter.24.cloned.1.call-start = ((), (), s32[]{:S(2)}) async-start(), calls=%async_computation.31 | async-start | bytes 10485760 | tf_op jit(solution)/shard_map/reduce_scatter | solution.py:119
  1018.4 262.2 %reduce-scatter.22.cloned.1.call-start = ((), (), s32[]{:S(2)}) async-start(), calls=%async_computation.29 | async-start | bytes 1310720 | tf_op jit(solution)/shard_map/reduce_scatter | solution.py:119
  1028.3 326.2 %reduce-scatter.18.cloned.1.call-start = ((), (), s32[]{:S(2)}) async-start(), calls=%async_computation.26 | async-start | bytes 9437184 | tf_op jit(solution)/shard_map/reduce_scatter | solution.py:101
  1040.9 389.0 %reduce-scatter.12.cloned.1.call-start = ((), (), s32[]{:S(2)}) async-start(), calls=%async_computation.21 | async-start | bytes 9437184 | tf_op jit(solution)/shard_map/reduce_scatter | solution.py:101
  1055.2 429.7 %reduce-scatter.20.cloned.1.call-start = ((), (), s32[]{:S(2)}) async-start(), calls=%async_computation.27 | async-start | bytes 1966080 | tf_op jit(solution)/shard_map/reduce_scatter | solution.py:119
  1064.4 478.5 %all-gather.44.cloned.1.call-start = ((), (), s32[]{:S(2)}) async-start(), calls=%async_computation.35 | async-start | bytes 5242880 | tf_op jit(solution)/shard_map/all_gather | solution.py:311
  1102.6 495.2 %all-gather.40.cloned.1.call-start = ((), (), s32[]{:S(2)}) async-start(), calls=%async_computation.32 | async-start | bytes 5242880 | tf_op jit(solution)/shard_map/all_gather | solution.py:308
  1253.6 399.3 %all-gather.42.cloned.1.call-start = ((), (), s32[]{:S(2)}) async-start(), calls=%async_computation.33 | async-start | bytes 5242880 | tf_op jit(solution)/shard_map/all_gather | solution.py:308
  1254.3 426.9 %all-gather.38.cloned.1.call-start = ((), (), s32[]{:S(2)}) async-start(), calls=%async_computation.30 | async-start | bytes 1310720 | tf_op jit(solution)/shard_map/all_gather | solution.py:311
  1440.1 272.8 %all-gather.36.cloned.1.call-start = ((), (), s32[]{:S(2)}) async-start(), calls=%async_computation.28 | async-start | bytes 1310720 | tf_op jit(solution)/shard_map/all_gather | solution.py:308
  1489.2 266.0 %all-to-all-start.3 = ((bf16[256,4,512]{2,0,1:T(8,128)(2,1)}), bf16[256,4,512]{2,0,1:T(8,128)(2,1)S(1)}, u32[]{:S(2)}, u32[]{:S(2)}) async-start(bf16[256,4,512]{2,0,1:T(8,128)(2,1)} %bitcast.272), calls=%async_computation.8 | async-start | bytes 2097152 | tf_op jit(solution)/shard_map/all_to_all | solution.py:111
  (39 other events, 3912.1 us)
Sparse Core Ops, SparseCore 0:
  16.6 48.6 all-gather.19
  67.8 53.4 all-gather.17
  130.3 46.2 all-gather.21
  178.6 26.1 all-gather.23
  247.2 69.6 reduce-scatter.9
  318.9 169.1 all-gather.27
  490.6 52.3 all-gather.25
  545.1 80.7 all-gather.29
  628.4 52.7 all-gather.31
  727.5 71.4 reduce-scatter.13
  803.9 54.2 all-gather.33
  980.6 43.6 reduce-scatter.15
  1026.5 75.9 reduce-scatter.25
  1105.3 145.1 reduce-scatter.23
  1252.6 27.8 reduce-scatter.21
  1284.4 70.0 reduce-scatter.17
  1358.4 71.4 reduce-scatter.11
  1432.6 52.2 reduce-scatter.19
  1486.8 56.1 all-gather.43
  1545.2 52.5 all-gather.39
  1600.3 52.5 all-gather.41
  1654.7 26.4 all-gather.37
  1683.1 28.7 all-gather.35
where the time goes:
time: 1770 us; the launch traced here: 1760 us
  waiting for transfers between devices  1120 us (63%)
  matrix products  297 us (17%)
  blocking collectives  175 us (10%)
  other arithmetic  82.7 us (5%)
  local copies, waits for them, and re-layouts  54.2 us (3%)
  starting transfers between devices  18.3 us (1%)
    reduce_scatter x4, waiting for transfers between devices, plane_scatter(): lax.psum_scatter(values.astype(jnp.bfloat16), PLANE, scatter_dimension=0,...  286 us
    reduce_scatter x5, waiting for transfers between devices, line_scatter(): lax.psum_scatter(values.astype(jnp.bfloat16), 'mx', scatter_dimension=axi...  257 us
    all_gather x4, waiting for transfers between devices, plane_gather(): return lax.all_gather(values, PLANE, axis=0, tiled=True)  220 us
    all_gather x5, waiting for transfers between devices, line_gather(): return lax.all_gather(values, 'mx', axis=axis, tiled=True)  191 us
    all_gather x3, waiting for transfers between devices, spread_cols(): return lax.all_gather(own, 'dp', axis=1, tiled=True).astype(jnp.float32)  96.4 us
    all_gather x2, waiting for transfers between devices, spread_rows(): return lax.all_gather(own, 'dp', axis=0, tiled=True).astype(jnp.float32)  69.4 us
    dot_general x4, matrix products, product(): lax.dot_general(left, weight, (((1,), (1,)), ((), ())), preferred_element...  59.1 us
    all_to_all x1, blocking collectives, to_rows(): return lax.all_to_all(values, 'mx', split_axis=0, concat_axis=1, tiled=True)  57.9 us
  transfers between devices with their start and end apart: 26, of which 20 were waited for; matrix products, arithmetic and copies ran while one was open for 13% of the time, Pallas kernels for 0%

commit v1 on v0

--- a/solution.py
+++ b/solution.py
@@ -104,7 +104,10 @@
 
 
 def to_rows(values):
-    return lax.all_to_all(values, "mx", split_axis=0, concat_axis=1, tiled=True)
+    return jnp.concatenate(
+        lax.all_to_all(jnp.stack(jnp.split(values, lax.axis_size("mx"), axis=0)), "mx", 0, 0),
+        axis=1,
+    )
 
 
 def to_tiles(values):

time: 1770 us -> 1770 us (level)
  no operation moved by 1% of the time
where the time goes in v1:
time: 1770 us
  waiting for transfers between devices  1120 us (63%)
  matrix products  297 us (17%)
  blocking collectives  176 us (10%)
  other arithmetic  83.9 us (5%)
  local copies, waits for them, and re-layouts  55.9 us (3%)
  starting transfers between devices  17.9 us (1%)
    reduce_scatter x4, waiting for transfers between devices, plane_scatter(): lax.psum_scatter(values.astype(jnp.bfloat16), PLANE, scatter_dimension=0,...  286 us
    reduce_scatter x5, waiting for transfers between devices, line_scatter(): lax.psum_scatter(values.astype(jnp.bfloat16), 'mx', scatter_dimension=axi...  257 us
    all_gather x4, waiting for transfers between devices, plane_gather(): return lax.all_gather(values, PLANE, axis=0, tiled=True)  220 us
    all_gather x5, waiting for transfers between devices, line_gather(): return lax.all_gather(values, 'mx', axis=axis, tiled=True)  191 us
    all_gather x3, waiting for transfers between devices, spread_cols(): return lax.all_gather(own, 'dp', axis=1, tiled=True).astype(jnp.float32)  96.4 us
    all_gather x2, waiting for transfers between devices, spread_rows(): return lax.all_gather(own, 'dp', axis=0, tiled=True).astype(jnp.float32)  69.4 us
    dot_general x4, matrix products, product(): lax.dot_general(left, weight, (((1,), (1,)), ((), ())), preferred_element...  59.2 us
    all_to_all x1, blocking collectives, to_rows(): lax.all_to_all(jnp.stack(jnp.split(values, lax.axis_size('mx'), axis=0)),...  58.3 us
  transfers between devices with their start and end apart: 26, of which 20 were waited for; matrix products, arithmetic and copies ran while one was open for 13% of the time, Pallas kernels for 0%

profile of v1, /device:TPU:0, one launch (start us, length us, event | category | flops | bytes accessed | tf_op | source)
XLA Modules:
  0.0 1768.0 jit_solution(5059973860310798623)
XLA Ops:
  17.3 46.3 %all_gather.61 = f32[2,2048]{1,0:T(2,128)S(1)} all-gather(f32[2,512]{1,0:T(2,128)S(1)} %pad_maximum_fusion.12), channel_id=1, replica_groups=mesh['dp'=4,'mx'=4,'my'=2] {'mx'}, dimensions={1}, use_global_device_ids=true | all-gather | bytes 20480 | tf_op jit(solution)/shard_map/all_gather | solution.py:118
  68.1 55.6 %all-gather.18.cloned.1.call-done = bf16[2048,2048]{1,0:T(8,128)(2,1)} async-done(((bf16[256,2048]{1,0:T(8,128)(2,1)}), bf16[2048,2048]{1,0:T(8,128)(2,1)}) %all-gather.18.cloned.1.call-update) | async-done | bytes 8388624 | tf_op jit(solution)/shard_map/all_gather | solution.py:97
  150.9 28.1 %all-gather.22.cloned.1.call-done = bf16[8,1024,128]{1,2,0:T(8,128)(2,1)} async-done(((bf16[8,256,128]{1,2,0:T(8,128)(2,1)}), bf16[8,1024,128]{1,2,0:T(8,128)(2,1)}) %all-gather.22.cloned.1.call-update) | async-done | bytes 2097168 | tf_op jit(solution)/shard_map/all_gather | solution.py:118
  182.1 57.7 %while.28 = (s32[]{:T(128)}, bf16[8,256,4,64]{1,3,2,0:T(8,128)(2,1)}, f32[8,256,4]{1,2,0:T(4,128)S(1)}, pred[8,256,1024]{2,1,0:T(8,128)(4,1)}, bf16[8,256,4,64]{...) while((s32[]{:T(128)}, bf16[8,256,4,64]{1,3,2,0:T(8,128)(2,1)}, ...), condition=%wide.region_6.7_spmd.clone, body=%wide.region_3.6_spmd.sunk.clone | while | flops 281017344 | bytes 14583893 | solution.py:242
  252.7 66.5 %reduce-scatter.10.cloned.1.call-done = bf16[256,2048]{1,0:T(8,128)(2,1)} async-done(((bf16[2048,2048]{1,0:T(8,128)(2,1)}), bf16[256,2048]{1,0:T(8,128)(2,1)}) %reduce-scatter.10.cloned.1.call-update) | async-done | bytes 1048592 | tf_op jit(solution)/shard_map/reduce_scatter | solution.py:101
  326.3 58.3 %all_to_all.48 = bf16[4,256,512]{2,1,0:T(8,128)(2,1)S(1)} all-to-all(bf16[4,256,512]{2,1,0:T(8,128)(2,1)S(1)} %pad_maximum_fusion.6), channel_id=1, replica_groups=mesh['dp'=4,'mx'=4,'my'=2] {'mx'}, dimensions={0} | all-to-all | bytes 2097152 | tf_op jit(solution)/shard_map/all_to_all | solution.py:108
  387.6 104.3 %all-gather.28.cloned.1.call-done = bf16[2048,2048]{1,0:T(8,128)(2,1)} async-done(((bf16[512,2048]{1,0:T(8,128)(2,1)}), bf16[2048,2048]{1,0:T(8,128)(2,1)}) %all-gather.28.cloned.1.call-update) | async-done | bytes 8388624 | tf_op jit(solution)/shard_map/all_gather | solution.py:118
  491.9 54.9 %all-gather.26.cloned.1.call-done = bf16[2048,2048]{1,0:T(8,128)(2,1)} async-done(((bf16[256,2048]{1,0:T(8,128)(2,1)}), bf16[2048,2048]{1,0:T(8,128)(2,1)}) %all-gather.26.cloned.1.call-update) | async-done | bytes 8388624 | tf_op jit(solution)/shard_map/all_gather | solution.py:97
  546.8 24.3 %fusion.93 = f32[2048,2048]{0,1:T(8,128)} fusion(bf16[2048,2048]{1,0:T(8,128)(2,1)} %all-gather.26.cloned.1.call-done, bf16[2048,2048]{1,0:T(8,128)(2,1)} %all-gather.28.cloned.1.call-done), kind=kOutput, calls=%fused_computation.193 | convolution fusion | flops 17179869184 | bytes 33554432 | tf_op jit(solution)/shard_map/dot_general | solution.py:45
  571.1 58.6 %all-gather.30.cloned.1.call-done = bf16[1024,2048]{1,0:T(8,128)(2,1)} async-done(((bf16[1024,512]{1,0:T(8,128)(2,1)}), bf16[1024,2048]{1,0:T(8,128)(2,1)}) %all-gather.30.cloned.1.call-update) | async-done | bytes 4194320 | tf_op jit(solution)/shard_map/all_gather | solution.py:118
  629.7 55.2 %all-gather.32.cloned.1.call-done = bf16[2048,2048]{1,0:T(8,128)(2,1)} async-done(((bf16[256,2048]{1,0:T(8,128)(2,1)}), bf16[2048,2048]{1,0:T(8,128)(2,1)}) %all-gather.32.cloned.1.call-update) | async-done | bytes 8388624 | tf_op jit(solution)/shard_map/all_gather | solution.py:97
  731.3 71.6 %reduce-scatter.14.cloned.1.call-done = bf16[256,2048]{1,0:T(8,128)(2,1)} async-done(((bf16[2048,2048]{1,0:T(8,128)(2,1)}), bf16[256,2048]{1,0:T(8,128)(2,1)}) %reduce-scatter.14.cloned.1.call-update) | async-done | bytes 1048592 | tf_op jit(solution)/shard_map/reduce_scatter | solution.py:101
  807.7 54.3 %all-gather.34.cloned.1.call-done = bf16[2048,2048]{1,0:T(8,128)(2,1)} async-done(((bf16[256,2048]{1,0:T(8,128)(2,1)}), bf16[2048,2048]{1,0:T(8,128)(2,1)}) %all-gather.34.cloned.1.call-update) | async-done | bytes 8388624 | tf_op jit(solution)/shard_map/all_gather | solution.py:97
  871.3 109.9 %while.29 = (s32[]{:T(128)}, f32[8,256,4,64]{1,3,2,0:T(8,128)}, bf16[8,1024,64]{1,2,0:T(8,128)(2,1)}, bf16[8,1024,64]{1,2,0:T(8,128)(2,1)}, pred[8,256,1024]{2,1...) while((s32[]{:T(128)}, f32[8,256,4,64]{1,3,2,0:T(8,128)}, ...), condition=%wide.region_14.15_spmd.clone, body=%wide.region_12.14_spmd.sunk.clone | while | flops 686947328 | bytes 34505836 | solution.py:282
  1068.3 38.0 %reduce-scatter.26.cloned.1.call-done = bf16[1024,512]{1,0:T(8,128)(2,1)} async-done(((bf16[1024,2048]{1,0:T(8,128)(2,1)}), bf16[1024,512]{1,0:T(8,128)(2,1)}) %reduce-scatter.26.cloned.1.call-update) | async-done | bytes 1048592 | tf_op jit(solution)/shard_map/reduce_scatter | solution.py:122
  1106.5 147.9 %reduce-scatter.24.cloned.1.call-done = bf16[512,2048]{1,0:T(8,128)(2,1)} async-done(((bf16[2048,2048]{1,0:T(8,128)(2,1)}), bf16[512,2048]{1,0:T(8,128)(2,1)}) %reduce-scatter.24.cloned.1.call-update) | async-done | bytes 2097168 | tf_op jit(solution)/shard_map/reduce_scatter | solution.py:122
  1258.2 26.2 %reduce-scatter.22.cloned.1.call-done = bf16[256,512]{1,0:T(8,128)(2,1)} async-done(((bf16[256,2048]{1,0:T(8,128)(2,1)}), bf16[256,512]{1,0:T(8,128)(2,1)}) %reduce-scatter.22.cloned.1.call-update) | async-done | bytes 262160 | tf_op jit(solution)/shard_map/reduce_scatter | solution.py:122
  1284.4 73.9 %reduce-scatter.18.cloned.1.call-done = bf16[256,2048]{1,0:T(8,128)(2,1)} async-done(((bf16[2048,2048]{1,0:T(8,128)(2,1)}), bf16[256,2048]{1,0:T(8,128)(2,1)}) %reduce-scatter.18.cloned.1.call-update) | async-done | bytes 1048592 | tf_op jit(solution)/shard_map/reduce_scatter | solution.py:101
  1360.2 73.5 %reduce-scatter.12.cloned.1.call-done = bf16[256,2048]{1,0:T(8,128)(2,1)} async-done(((bf16[2048,2048]{1,0:T(8,128)(2,1)}), bf16[256,2048]{1,0:T(8,128)(2,1)}) %reduce-scatter.12.cloned.1.call-update) | async-done | bytes 1048592 | tf_op jit(solution)/shard_map/reduce_scatter | solution.py:101
  1443.9 44.9 %reduce-scatter.20.cloned.1.call-done = bf16[512,384]{1,0:T(8,128)(2,1)} async-done(((bf16[2048,384]{1,0:T(8,128)(2,1)}), bf16[512,384]{1,0:T(8,128)(2,1)}) %reduce-scatter.20.cloned.1.call-update) | async-done | bytes 393232 | tf_op jit(solution)/shard_map/reduce_scatter | solution.py:122
  1499.1 47.7 %all-gather.44.cloned.1.call-done = bf16[4096,512]{1,0:T(8,128)(2,1)} async-done(((bf16[1024,512]{1,0:T(8,128)(2,1)}), bf16[4096,512]{1,0:T(8,128)(2,1)}) %all-gather.44.cloned.1.call-update) | async-done | bytes 4194320 | tf_op jit(solution)/shard_map/all_gather | solution.py:314
  1553.6 48.1 %all-gather.40.cloned.1.call-done = bf16[512,4096]{1,0:T(8,128)(2,1)} async-done(((bf16[512,1024]{1,0:T(8,128)(2,1)}), bf16[512,4096]{1,0:T(8,128)(2,1)}) %all-gather.40.cloned.1.call-update) | async-done | bytes 4194320 | tf_op jit(solution)/shard_map/all_gather | solution.py:311
  1608.3 48.4 %all-gather.42.cloned.1.call-done = bf16[512,4096]{1,0:T(8,128)(2,1)} async-done(((bf16[512,1024]{1,0:T(8,128)(2,1)}), bf16[512,4096]{1,0:T(8,128)(2,1)}) %all-gather.42.cloned.1.call-update) | async-done | bytes 4194320 | tf_op jit(solution)/shard_map/all_gather | solution.py:311
  1719.5 38.9 %psum.7 = f32[2,2048]{1,0:T(2,128)S(1)} all-reduce(f32[2,2048]{1,0:T(2,128)S(1)} %pad_maximum_fusion.11), channel_id=1, replica_groups=mesh['dp'=4,'mx'=4,'my'=2] {'dp','mx','my'}, use_global_device_ids=true, to_apply=%region_20.21 | all-reduce | flops 4096 | bytes 32768 | tf_op jit(solution)/shard_map/psum | solution.py:330
  (350 shorter events, 487.0 us)
Async XLA Ops:
  9.7 53.8 %all-to-all-start = ((bf16[4,256,512]{2,1,0:T(8,128)(2,1)}), bf16[4,256,512]{2,1,0:T(8,128)(2,1)S(1)}, u32[]{:S(2)}, u32[]{:S(2)}) async-start(bf16[4,256,512]{2,1,0:T(8,128)(2,1)} %pad_maximum_fusion.5), calls=%async_computation | async-start | bytes 2097152 | tf_op jit(solution)/shard_map/all_to_all | solution.py:108
  17.2 106.5 %all-gather.18.cloned.1.call-start = ((), (), s32[]{:S(2)}) async-start(), calls=%async_computation.13 | async-start | bytes 9437184 | tf_op jit(solution)/shard_map/all_gather | solution.py:97
  67.7 111.2 %all-gather.22.cloned.1.call-start = ((), (), s32[]{:S(2)}) async-start(), calls=%async_computation.15 | async-start | bytes 2621440 | tf_op jit(solution)/shard_map/all_gather | solution.py:118
  132.6 109.4 %all-gather.24.cloned.1.call-start = ((), (), s32[]{:S(2)}) async-start(), calls=%async_computation.16 | async-start | bytes 1310720 | tf_op jit(solution)/shard_map/all_gather | solution.py:118
  134.3 184.9 %reduce-scatter.10.cloned.1.call-start = ((), (), s32[]{:S(2)}) async-start(), calls=%async_computation.17 | async-start | bytes 9437184 | tf_op jit(solution)/shard_map/reduce_scatter | solution.py:101
  249.4 242.6 %all-gather.28.cloned.1.call-start = ((), (), s32[]{:S(2)}) async-start(), calls=%async_computation.19 | async-start | bytes 10485760 | tf_op jit(solution)/shard_map/all_gather | solution.py:118
  252.7 294.1 %all-gather.26.cloned.1.call-start = ((), (), s32[]{:S(2)}) async-start(), calls=%async_computation.18 | async-start | bytes 9437184 | tf_op jit(solution)/shard_map/all_gather | solution.py:97
  322.5 307.3 %all-gather.30.cloned.1.call-start = ((), (), s32[]{:S(2)}) async-start(), calls=%async_computation.20 | async-start | bytes 5242880 | tf_op jit(solution)/shard_map/all_gather | solution.py:118
  324.8 360.2 %all-gather.32.cloned.1.call-start = ((), (), s32[]{:S(2)}) async-start(), calls=%async_computation.22 | async-start | bytes 9437184 | tf_op jit(solution)/shard_map/all_gather | solution.py:97
  387.6 415.3 %reduce-scatter.14.cloned.1.call-start = ((), (), s32[]{:S(2)}) async-start(), calls=%async_computation.23 | async-start | bytes 9437184 | tf_op jit(solution)/shard_map/reduce_scatter | solution.py:101
  731.2 130.8 %all-gather.34.cloned.1.call-start = ((), (), s32[]{:S(2)}) async-start(), calls=%async_computation.24 | async-start | bytes 9437184 | tf_op jit(solution)/shard_map/all_gather | solution.py:97
  807.6 227.7 %reduce-scatter.16.cloned.1.call-start = ((), (), s32[]{:S(2)}) async-start(), calls=%async_computation.25 | async-start | bytes 2621440 | tf_op jit(solution)/shard_map/reduce_scatter | solution.py:122
  984.3 122.1 %reduce-scatter.26.cloned.1.call-start = ((), (), s32[]{:S(2)}) async-start(), calls=%async_computation.34 | async-start | bytes 5242880 | tf_op jit(solution)/shard_map/reduce_scatter | solution.py:122
  998.2 256.1 %reduce-scatter.24.cloned.1.call-start = ((), (), s32[]{:S(2)}) async-start(), calls=%async_computation.31 | async-start | bytes 10485760 | tf_op jit(solution)/shard_map/reduce_scatter | solution.py:122
  1022.2 262.2 %reduce-scatter.22.cloned.1.call-start = ((), (), s32[]{:S(2)}) async-start(), calls=%async_computation.29 | async-start | bytes 1310720 | tf_op jit(solution)/shard_map/reduce_scatter | solution.py:122
  1032.1 326.2 %reduce-scatter.18.cloned.1.call-start = ((), (), s32[]{:S(2)}) async-start(), calls=%async_computation.26 | async-start | bytes 9437184 | tf_op jit(solution)/shard_map/reduce_scatter | solution.py:101
  1044.8 389.0 %reduce-scatter.12.cloned.1.call-start = ((), (), s32[]{:S(2)}) async-start(), calls=%async_computation.21 | async-start | bytes 9437184 | tf_op jit(solution)/shard_map/reduce_scatter | solution.py:101
  1059.1 429.7 %reduce-scatter.20.cloned.1.call-start = ((), (), s32[]{:S(2)}) async-start(), calls=%async_computation.27 | async-start | bytes 1966080 | tf_op jit(solution)/shard_map/reduce_scatter | solution.py:122
  1068.3 478.5 %all-gather.44.cloned.1.call-start = ((), (), s32[]{:S(2)}) async-start(), calls=%async_computation.35 | async-start | bytes 5242880 | tf_op jit(solution)/shard_map/all_gather | solution.py:314
  1106.4 495.2 %all-gather.40.cloned.1.call-start = ((), (), s32[]{:S(2)}) async-start(), calls=%async_computation.32 | async-start | bytes 5242880 | tf_op jit(solution)/shard_map/all_gather | solution.py:311
  1257.4 399.3 %all-gather.42.cloned.1.call-start = ((), (), s32[]{:S(2)}) async-start(), calls=%async_computation.33 | async-start | bytes 5242880 | tf_op jit(solution)/shard_map/all_gather | solution.py:311
  1258.1 426.9 %all-gather.38.cloned.1.call-start = ((), (), s32[]{:S(2)}) async-start(), calls=%async_computation.30 | async-start | bytes 1310720 | tf_op jit(solution)/shard_map/all_gather | solution.py:314
  1443.9 272.8 %all-gather.36.cloned.1.call-start = ((), (), s32[]{:S(2)}) async-start(), calls=%async_computation.28 | async-start | bytes 1310720 | tf_op jit(solution)/shard_map/all_gather | solution.py:311
  1493.0 266.0 %all-to-all-start.3 = ((bf16[256,4,512]{2,0,1:T(8,128)(2,1)}), bf16[256,4,512]{2,0,1:T(8,128)(2,1)S(1)}, u32[]{:S(2)}, u32[]{:S(2)}) async-start(bf16[256,4,512]{2,0,1:T(8,128)(2,1)} %bitcast.286), calls=%async_computation.8 | async-start | bytes 2097152 | tf_op jit(solution)/shard_map/all_to_all | solution.py:114
  (41 other events, 3936.7 us)
Sparse Core Ops, SparseCore 0:
  19.0 48.6 all-gather.19
  70.2 53.4 all-gather.17
  132.7 46.2 all-gather.21
  181.0 26.1 all-gather.23
  249.5 69.6 reduce-scatter.9
  321.2 170.6 all-gather.27
  494.4 52.3 all-gather.25
  548.9 80.7 all-gather.29
  632.2 52.7 all-gather.31
  731.3 71.4 reduce-scatter.13
  807.7 54.2 all-gather.33
  984.4 43.6 reduce-scatter.15
  1030.3 75.9 reduce-scatter.25
  1109.1 145.1 reduce-scatter.23
  1256.5 27.8 reduce-scatter.21
  1288.3 70.0 reduce-scatter.17
  1362.2 71.4 reduce-scatter.11
  1436.5 52.2 reduce-scatter.19
  1490.6 56.1 all-gather.43
  1549.0 52.5 all-gather.39
  1604.1 52.5 all-gather.41
  1658.5 26.4 all-gather.37
  1686.9 28.7 all-gather.35
